TPU v7x, 32 devices: a whole 2x2x4 slice. The times are simulated.
32 devices in a mesh: pair: 16 (over z, y, x), rep: 2 (over core).
Axes of the slice: x: 2, y: 2, z: 4, core: 2. Of those that a mesh axis runs over, the one named last changes fastest.
Arguments:
- triplet_pairs: int32 [256, 3], P(('pair', 'rep')), may hold values from 0 to 1023, as said below
- tno_width: int32 [256], P(('pair', 'rep')), may hold values from 64 to 128
- pair_width: int32 [1024], P('pair'), may hold values from 32 to 64
- pair_coeff: bfloat16 [1024, 64, 1024], P('pair'), may hold values from -0.1875 to 0.1875
- pair_amps: bfloat16 [1024, 64, 64], P('pair'), may hold values from -0.03125 to 0.03125
- pair_exch: bfloat16 [1024, 64, 64], P('pair'), may hold values from -0.3125 to 0.3125
- tno_coeff: bfloat16 [256, 1024, 128], P(('pair', 'rep')), may hold values from -0.1875 to 0.1875
- int_left: bfloat16 [256, 3, 128, 128], P(('pair', 'rep')), may hold values from -6 to 6
- int_right: bfloat16 [256, 3, 128, 128], P(('pair', 'rep')), may hold values from -6 to 6
- singles: float32 [256, 3, 128], P(('pair', 'rep')), may hold values from -6 to 6
- tno_energy: float32 [256, 128], P(('pair', 'rep')), may hold values from 0.5 to 5
- gap: float32 [256], P(('pair', 'rep')), may hold values from 1 to 4
Outputs:
- triplet_energy: float32 [256], P(('pair', 'rep'))
- pair_energy: float32 [1024], P('pair')
Inputs may be any that keep to these rules, and one draw needn't show every extreme that they name: `triplet_pairs`: pair p is owned by index p // 64 of axis pair. The triplets of one chip are rows 2 * c * 8 to 2 * (c + 1) * 8 - 1; among their 48 pair ids at most 3 have one owner, and in every chip some owner has exactly 3 of them.
All inputs are finite; a program needn't handle non-finite values.
Results may differ from a plain program's by a relative error of at most 0.00044.
Values may be sent and summed in bfloat16 or wider, within the bound.
A program may use at most 128 MiB of HBM per device.

v0:
```python
import jax
import jax.numpy as jnp
from jax import lax
from jax.sharding import PartitionSpec as P


def projected_energy(
    pno_coeff, pno_blocks, tno_block, tno_count, left, right, single_amps, tno_levels, shift
):
    tno_size = tno_block.shape[1]
    pno_size = pno_coeff.shape[1]
    kept_cols = (jnp.arange(tno_size, dtype=jnp.int32) < tno_count).astype(jnp.float32)
    tno_kept = tno_block * kept_cols.astype(jnp.bfloat16)[None, :]
    intersection = jnp.einsum(
        "xad,db->xab", pno_coeff, tno_kept, preferred_element_type=jnp.float32
    ).astype(jnp.bfloat16)
    halfway = jnp.einsum(
        "xab,xac->xbc", intersection, pno_blocks, preferred_element_type=jnp.float32
    ).astype(jnp.bfloat16)
    halfway = halfway.reshape(3, tno_size, 2, pno_size)
    projected = jnp.einsum(
        "xbkc,xcd->xkbd", halfway, intersection, preferred_element_type=jnp.float32
    )
    amps_tno = projected[:, 0].astype(jnp.bfloat16)
    exch_tno = projected[:, 1]
    left_cols = jnp.transpose(left, (2, 0, 1)).reshape(tno_size, 3 * tno_size)
    right_cols = jnp.transpose(right, (2, 0, 1)).reshape(tno_size, 3 * tno_size)
    khatri = (left_cols[:, None, :] * right_cols[None, :, :]).reshape(
        tno_size * tno_size, 3 * tno_size
    )
    leading = jnp.transpose(amps_tno, (1, 0, 2)).reshape(tno_size, 3 * tno_size)
    connected = lax.dot_general(
        leading, khatri, (((1,), (1,)), ((), ())), preferred_element_type=jnp.float32
    )
    connected = connected.reshape(tno_size, tno_size, tno_size)
    complete = connected + single_amps[0][None, None, :] * exch_tno[0][:, :, None]
    complete = complete + single_amps[1][None, :, None] * exch_tno[1][:, None, :]
    complete = complete + single_amps[2][:, None, None] * exch_tno[2][None, :, :]
    denominator = (
        tno_levels[:, None, None] + tno_levels[None, :, None] + tno_levels[None, None, :] + shift
    )
    cube_mask = kept_cols[:, None, None] * kept_cols[None, :, None] * kept_cols[None, None, :]
    return jnp.sum(cube_mask * connected * complete / denominator)


def owner_ranks(owners):
    matching = owners[:, None] == owners[None, :]
    position = jnp.arange(owners.shape[0], dtype=jnp.int32)
    earlier = position[None, :] < position[:, None]
    return jnp.sum(jnp.logical_and(matching, earlier), axis=1)


def body(
    triplet_pairs,
    tno_width,
    pair_width,
    pair_coeff,
    pair_amps,
    pair_exch,
    tno_coeff,
    int_left,
    int_right,
    singles,
    tno_energy,
    gap,
):
    owner_count = lax.axis_size("pair")
    pair_dev = pair_coeff.shape[0]
    pno_size = pair_coeff.shape[1]
    domain = pair_coeff.shape[2]
    references = triplet_pairs.reshape(-1)
    ref_count = references.shape[0]
    capacity = (2 * ref_count + owner_count - 1) // owner_count
    kept_rows = (jnp.arange(pno_size, dtype=jnp.int32)[None, :] < pair_width[:, None]).astype(
        jnp.bfloat16
    )
    masked = pair_coeff * kept_rows[:, :, None]
    paired = jnp.concatenate([pair_amps, pair_exch], axis=2)
    chip_refs = lax.all_gather(references, "rep", axis=0, tiled=True)
    owners = chip_refs // pair_dev
    slot_rank = owner_ranks(owners)
    requests = (
        jnp.zeros((owner_count * capacity,), jnp.int32)
        .at[owners * capacity + slot_rank]
        .set(chip_refs % pair_dev)
    )
    requests = requests.reshape(owner_count, capacity)
    asked_rows = lax.all_to_all(requests, "pair", split_axis=0, concat_axis=0, tiled=True)
    replica = lax.axis_index("rep")
    coeff_part = lax.dynamic_slice_in_dim(masked, replica * (domain // 2), domain // 2, 2)
    paired_part = lax.dynamic_slice_in_dim(paired, replica * pno_size, pno_size, 2)
    got_coeff, got_paired = (
        lax.all_to_all(coeff_part[asked_rows], "pair", split_axis=0, concat_axis=0, tiled=True),
        lax.all_to_all(paired_part[asked_rows], "pair", split_axis=0, concat_axis=0, tiled=True),
    )
    got_coeff, got_paired = (
        lax.all_gather(got_coeff, "rep", axis=3, tiled=True),
        lax.all_gather(got_paired, "rep", axis=3, tiled=True),
    )
    positions = owners * capacity + slot_rank
    positions = lax.dynamic_slice_in_dim(positions, replica * ref_count, ref_count)
    flat_coeff = got_coeff.reshape(-1, pno_size, domain)
    flat_paired = got_paired.reshape(-1, pno_size, 2 * pno_size)
    trips = tno_coeff.shape[0]
    coeff_trip = flat_coeff[positions].reshape(trips, 3, pno_size, domain)
    paired_trip = flat_paired[positions].reshape(trips, 3, pno_size, 2 * pno_size)

    def single_triplet(items):
        return projected_energy(*items)

    energies = lax.map(
        single_triplet,
        (
            coeff_trip,
            paired_trip,
            tno_coeff,
            tno_width,
            int_left,
            int_right,
            singles,
            tno_energy,
            gap,
        ),
    )
    shares = jnp.repeat(energies / 3.0, 3)
    all_pairs = jnp.arange(owner_count * pair_dev, dtype=jnp.int32)
    dense = jnp.sum(
        jnp.where(references[:, None] == all_pairs[None, :], shares[:, None], 0.0), axis=0
    )
    owned = lax.psum_scatter(dense, "pair", scatter_dimension=0, tiled=True)
    pair_energy = lax.psum(owned, "rep")
    return (energies, pair_energy)


def solution(mesh):
    placed = (
        P(("pair", "rep"), None),
        P(("pair", "rep")),
        P("pair"),
        P("pair", None, None),
        P("pair", None, None),
        P("pair", None, None),
        P(("pair", "rep"), None, None),
        P(("pair", "rep"), None, None, None),
        P(("pair", "rep"), None, None, None),
        P(("pair", "rep"), None, None),
        P(("pair", "rep"), None),
        P(("pair", "rep")),
    )
    return jax.shard_map(
        body, mesh=mesh, in_specs=placed, out_specs=(P(("pair", "rep")), P("pair")), check_vma=False
    )
```

profile of v0, /device:TPU:0, one launch (start us, length us, event | category | flops | bytes accessed | tf_op | source)
XLA Modules:
  0.0 362.0 jit_solution(6125471141535542919)
XLA Ops:
  8.0 1.2 dynamic-slice
  10.2 2.0 all-reduce
  13.7 8.2 %all-to-all-start = ((s32[16,1,3]{2,1,0:T(1,128)}), s32[16,1,3]{2,1,0:T(1,128)S(1)}, u32[]{:S(2)}, u32[]{:S(2)}) async-start(s32[16,1,3]{2,1,0:T(1,128)} %bitcast.29), calls=%async_computation | async-start | bytes 16384 | tf_op jit(solution)/shard_map/all_to_all | solution.py:88
  22.7 4.0 %dynamic-slice_multiply_fusion = bf16[64,64,512]{2,1,0:T(8,128)(2,1)} fusion(bf16[64,64,1024]{2,1,0:T(8,128)(2,1)} %param.17, s32[]{:T(128)S(6)} %select_n.43, bf16[64,64]{1,0:T(8,128)(2,1)S(1)} %fusion.23), kind=kLoop, calls=%fused_computation.43 | loop fusion | flops 8388608 | bytes 8396804 | tf_op jit(solution)/shard_map/mul | solution.py:77
  26.7 2.5 all-to-all-done
  29.5 2.9 gather_fusion
  32.5 75.4 %all_to_all.22 = bf16[16,3,64,512]{3,2,1,0:T(8,128)(2,1)} all-to-all(bf16[16,3,64,512]{3,2,1,0:T(8,128)(2,1)S(1)} %bitcast.110), channel_id=1, replica_groups=mesh['pair'=16,'rep'=2] {'pair'}, dimensions={0} | all-to-all | bytes 6291456 | tf_op jit(solution)/shard_map/all_to_all | solution.py:93
  107.9 2.6 dynamic-slice_maximum_fusion
  111.2 1.3 reshape.272
  112.5 3.9 %all-to-all-start.2 = ((bf16[16,2,6144]{2,1,0:T(2,128)(2,1)}), bf16[16,2,6144]{2,1,0:T(2,128)(2,1)S(1)}, u32[]{:S(2)}, u32[]{:S(2)}) async-start(bf16[16,2,6144]{2,1,0:T(2,128)(2,1)} %reshape.272), calls=%async_computation.2 | async-start | bytes 786432 | tf_op jit(solution)/shard_map/all_to_all | solution.py:94
  117.8 10.5 %all-to-all-done.2 = bf16[16,2,6144]{2,1,0:T(2,128)(2,1)S(1)} async-done(((bf16[16,2,6144]{2,1,0:T(2,128)(2,1)}), bf16[16,2,6144]{2,1,0:T(2,128)(2,1)S(1)}, u32[]{:S(2)}, u32[]{:S(2)}) %all-to-all-start.2) | async-done | bytes 393248 | tf_op jit(solution)/shard_map/all_to_all | solution.py:94
  129.5 2.9 all_gather.11
  133.6 1.4 gather_fusion.3
  134.9 3.5 gather_fusion.1
  138.5 174.5 %while.10 = (s32[]{:T(128)}, f32[8]{0:T(128)S(1)}, s32[8]{0:T(128)S(1)}, bf16[8,3,64,1024]{3,2,1,0:T(8,128)(2,1)S(1)}, bf16[8,1024,128]{2,1,0:T(8,128)(2,1)}, /*...) while((s32[]{:T(128)}, f32[8]{0:T(128)S(1)}, ...), condition=%wide.region_4.5_spmd, body=%wide.region_2.4_spmd.sunk | while | flops 1732485504 | bytes 29010464 | solution.py:111
  147.9 11.6 %fusion.51 = f32[]{:T(128)} fusion(f32[]{:T(128)} %bitcast.103, f32[128]{0:T(128)S(1)} %fusion.49, f32[128,128]{0,1:T(8,128)S(1)} %broadcast_add_fusion.2, f32[128,128]{1,0:T(8,128)S(1)} %copy.77, f32[128]{0:T(128)S(1)} %get-tuple-element.230, f32[128,128]{1,0:T(8,128)} %copy.78, f32[128]{0:T(128)S(1)} %get-tuple-element.232, ...), kind=kOutput, calls=%fused_computation.8.clone.1 | convolution fusion | flops 1663041536 | bytes 625160 | tf_op jit(solution)/shard_map/while/body/eval_jaxpr/dot_general | solution.py:32
  161.7 1.2 convolution_convert_fusion.4
  169.8 11.6 %fusion.51 = f32[]{:T(128)} fusion(f32[]{:T(128)} %bitcast.103, f32[128]{0:T(128)S(1)} %fusion.49, f32[128,128]{0,1:T(8,128)S(1)} %broadcast_add_fusion.2, f32[128,128]{1,0:T(8,128)S(1)} %copy.77, f32[128]{0:T(128)S(1)} %get-tuple-element.230, f32[128,128]{1,0:T(8,128)} %copy.78, f32[128]{0:T(128)S(1)} %get-tuple-element.232, ...), kind=kOutput, calls=%fused_computation.8.clone.1 | convolution fusion | flops 1663041536 | bytes 625160 | tf_op jit(solution)/shard_map/while/body/eval_jaxpr/dot_general | solution.py:32
  183.5 1.2 convolution_convert_fusion.4
  191.6 11.6 %fusion.51 = f32[]{:T(128)} fusion(f32[]{:T(128)} %bitcast.103, f32[128]{0:T(128)S(1)} %fusion.49, f32[128,128]{0,1:T(8,128)S(1)} %broadcast_add_fusion.2, f32[128,128]{1,0:T(8,128)S(1)} %copy.77, f32[128]{0:T(128)S(1)} %get-tuple-element.230, f32[128,128]{1,0:T(8,128)} %copy.78, f32[128]{0:T(128)S(1)} %get-tuple-element.232, ...), kind=kOutput, calls=%fused_computation.8.clone.1 | convolution fusion | flops 1663041536 | bytes 625160 | tf_op jit(solution)/shard_map/while/body/eval_jaxpr/dot_general | solution.py:32
  205.3 1.2 convolution_convert_fusion.4
  213.4 11.6 %fusion.51 = f32[]{:T(128)} fusion(f32[]{:T(128)} %bitcast.103, f32[128]{0:T(128)S(1)} %fusion.49, f32[128,128]{0,1:T(8,128)S(1)} %broadcast_add_fusion.2, f32[128,128]{1,0:T(8,128)S(1)} %copy.77, f32[128]{0:T(128)S(1)} %get-tuple-element.230, f32[128,128]{1,0:T(8,128)} %copy.78, f32[128]{0:T(128)S(1)} %get-tuple-element.232, ...), kind=kOutput, calls=%fused_computation.8.clone.1 | convolution fusion | flops 1663041536 | bytes 625160 | tf_op jit(solution)/shard_map/while/body/eval_jaxpr/dot_general | solution.py:32
  227.1 1.2 convolution_convert_fusion.4
  235.2 11.6 %fusion.51 = f32[]{:T(128)} fusion(f32[]{:T(128)} %bitcast.103, f32[128]{0:T(128)S(1)} %fusion.49, f32[128,128]{0,1:T(8,128)S(1)} %broadcast_add_fusion.2, f32[128,128]{1,0:T(8,128)S(1)} %copy.77, f32[128]{0:T(128)S(1)} %get-tuple-element.230, f32[128,128]{1,0:T(8,128)} %copy.78, f32[128]{0:T(128)S(1)} %get-tuple-element.232, ...), kind=kOutput, calls=%fused_computation.8.clone.1 | convolution fusion | flops 1663041536 | bytes 625160 | tf_op jit(solution)/shard_map/while/body/eval_jaxpr/dot_general | solution.py:32
  248.9 1.2 convolution_convert_fusion.4
  257.0 11.6 %fusion.51 = f32[]{:T(128)} fusion(f32[]{:T(128)} %bitcast.103, f32[128]{0:T(128)S(1)} %fusion.49, f32[128,128]{0,1:T(8,128)S(1)} %broadcast_add_fusion.2, f32[128,128]{1,0:T(8,128)S(1)} %copy.77, f32[128]{0:T(128)S(1)} %get-tuple-element.230, f32[128,128]{1,0:T(8,128)} %copy.78, f32[128]{0:T(128)S(1)} %get-tuple-element.232, ...), kind=kOutput, calls=%fused_computation.8.clone.1 | convolution fusion | flops 1663041536 | bytes 625160 | tf_op jit(solution)/shard_map/while/body/eval_jaxpr/dot_general | solution.py:32
  270.7 1.2 convolution_convert_fusion.4
  278.8 11.6 %fusion.51 = f32[]{:T(128)} fusion(f32[]{:T(128)} %bitcast.103, f32[128]{0:T(128)S(1)} %fusion.49, f32[128,128]{0,1:T(8,128)S(1)} %broadcast_add_fusion.2, f32[128,128]{1,0:T(8,128)S(1)} %copy.77, f32[128]{0:T(128)S(1)} %get-tuple-element.230, f32[128,128]{1,0:T(8,128)} %copy.78, f32[128]{0:T(128)S(1)} %get-tuple-element.232, ...), kind=kOutput, calls=%fused_computation.8.clone.1 | convolution fusion | flops 1663041536 | bytes 625160 | tf_op jit(solution)/shard_map/while/body/eval_jaxpr/dot_general | solution.py:32
  292.6 1.2 convolution_convert_fusion.4
  300.6 11.6 %fusion.51 = f32[]{:T(128)} fusion(f32[]{:T(128)} %bitcast.103, f32[128]{0:T(128)S(1)} %fusion.49, f32[128,128]{0,1:T(8,128)S(1)} %broadcast_add_fusion.2, f32[128,128]{1,0:T(8,128)S(1)} %copy.77, f32[128]{0:T(128)S(1)} %get-tuple-element.230, f32[128,128]{1,0:T(8,128)} %copy.78, f32[128]{0:T(128)S(1)} %get-tuple-element.232, ...), kind=kOutput, calls=%fused_computation.8.clone.1 | convolution fusion | flops 1663041536 | bytes 625160 | tf_op jit(solution)/shard_map/while/body/eval_jaxpr/dot_general | solution.py:32
  313.3 38.8 %all-reduce.1 = f32[1024]{0:T(1024)S(1)} all-reduce(f32[1024]{0:T(1024)S(1)} %select_reduce_fusion), channel_id=2, replica_groups=mesh['pair'=16,'rep'=2] {'pair'}, use_global_device_ids=true, to_apply=%region_6.7.clone | all-reduce | flops 1024 | bytes 8192
  352.2 2.9 psum.7
  (208 shorter events, 80.0 us)
Async XLA Ops:
  13.7 15.5 %all-to-all-start = ((s32[16,1,3]{2,1,0:T(1,128)}), s32[16,1,3]{2,1,0:T(1,128)S(1)}, u32[]{:S(2)}, u32[]{:S(2)}) async-start(s32[16,1,3]{2,1,0:T(1,128)} %bitcast.29), calls=%async_computation | async-start | bytes 16384 | tf_op jit(solution)/shard_map/all_to_all | solution.py:88
  21.9 113.0 %all-gather.2.cloned.1.call-start = ((), (), s32[]{:S(2)}) async-start(), calls=%async_computation.3 | async-start | bytes 9437184 | tf_op jit(solution)/shard_map/all_gather | solution.py:97
  32.5 84.0 %copy-start.4 = (u32[32]{0:T(128)S(1)}, u32[32]{0:T(128)}, u32[]{:S(2)}) copy-start(u32[32]{0:T(128)} %constant.93) | copy-start | bytes 388
  111.2 27.3 %copy-start.2 = (s32[8]{0:T(128)S(1)}, s32[8]{0:T(128)}, u32[]{:S(2)}) copy-start(s32[8]{0:T(128)} %param.15) | copy-start | bytes 100
  111.2 27.3 %copy-start.3 = (f32[8]{0:T(128)S(1)}, f32[8]{0:T(128)}, u32[]{:S(2)}) copy-start(f32[8]{0:T(128)} %param.25) | copy-start | bytes 100
  112.5 15.8 %all-to-all-start.2 = ((bf16[16,2,6144]{2,1,0:T(2,128)(2,1)}), bf16[16,2,6144]{2,1,0:T(2,128)(2,1)S(1)}, u32[]{:S(2)}, u32[]{:S(2)}) async-start(bf16[16,2,6144]{2,1,0:T(2,128)(2,1)} %reshape.272), calls=%async_computation.2 | async-start | bytes 786432 | tf_op jit(solution)/shard_map/all_to_all | solution.py:94
  138.5 3.6 %copy-start = (bf16[8,3,64,1024]{3,2,1,0:T(8,128)(2,1)}, bf16[8,3,64,1024]{3,2,1,0:T(8,128)(2,1)S(1)}, u32[]{:S(2)}) copy-start(bf16[8,3,64,1024]{3,2,1,0:T(8,128)(2,1)S(1)} %get-tuple-element.271) | copy-start | bytes 9437188 | tf_op jit(solution)/shard_map/while
  147.9 12.4 %copy-start.1 = (bf16[8,3,64,1024]{3,2,1,0:T(8,128)(2,1)S(1)}, bf16[8,3,64,1024]{3,2,1,0:T(8,128)(2,1)}, u32[]{:S(2)}) copy-start(bf16[8,3,64,1024]{3,2,1,0:T(8,128)(2,1)} %copy-done) | copy-start | bytes 9437188 | tf_op jit(solution)/shard_map/while
  160.3 3.6 copy-start
  169.8 12.4 %copy-start.1 = (bf16[8,3,64,1024]{3,2,1,0:T(8,128)(2,1)S(1)}, bf16[8,3,64,1024]{3,2,1,0:T(8,128)(2,1)}, u32[]{:S(2)}) copy-start(bf16[8,3,64,1024]{3,2,1,0:T(8,128)(2,1)} %copy-done) | copy-start | bytes 9437188 | tf_op jit(solution)/shard_map/while
  182.2 3.6 copy-start
  191.6 12.4 %copy-start.1 = (bf16[8,3,64,1024]{3,2,1,0:T(8,128)(2,1)S(1)}, bf16[8,3,64,1024]{3,2,1,0:T(8,128)(2,1)}, u32[]{:S(2)}) copy-start(bf16[8,3,64,1024]{3,2,1,0:T(8,128)(2,1)} %copy-done) | copy-start | bytes 9437188 | tf_op jit(solution)/shard_map/while
  204.0 3.6 copy-start
  213.4 12.4 %copy-start.1 = (bf16[8,3,64,1024]{3,2,1,0:T(8,128)(2,1)S(1)}, bf16[8,3,64,1024]{3,2,1,0:T(8,128)(2,1)}, u32[]{:S(2)}) copy-start(bf16[8,3,64,1024]{3,2,1,0:T(8,128)(2,1)} %copy-done) | copy-start | bytes 9437188 | tf_op jit(solution)/shard_map/while
  225.8 3.6 copy-start
  235.2 12.4 %copy-start.1 = (bf16[8,3,64,1024]{3,2,1,0:T(8,128)(2,1)S(1)}, bf16[8,3,64,1024]{3,2,1,0:T(8,128)(2,1)}, u32[]{:S(2)}) copy-start(bf16[8,3,64,1024]{3,2,1,0:T(8,128)(2,1)} %copy-done) | copy-start | bytes 9437188 | tf_op jit(solution)/shard_map/while
  247.6 3.6 copy-start
  257.0 12.4 %copy-start.1 = (bf16[8,3,64,1024]{3,2,1,0:T(8,128)(2,1)S(1)}, bf16[8,3,64,1024]{3,2,1,0:T(8,128)(2,1)}, u32[]{:S(2)}) copy-start(bf16[8,3,64,1024]{3,2,1,0:T(8,128)(2,1)} %copy-done) | copy-start | bytes 9437188 | tf_op jit(solution)/shard_map/while
  269.4 3.6 copy-start
  278.8 12.4 %copy-start.1 = (bf16[8,3,64,1024]{3,2,1,0:T(8,128)(2,1)S(1)}, bf16[8,3,64,1024]{3,2,1,0:T(8,128)(2,1)}, u32[]{:S(2)}) copy-start(bf16[8,3,64,1024]{3,2,1,0:T(8,128)(2,1)} %copy-done) | copy-start | bytes 9437188 | tf_op jit(solution)/shard_map/while
  291.2 3.6 copy-start
  300.6 12.4 %copy-start.1 = (bf16[8,3,64,1024]{3,2,1,0:T(8,128)(2,1)S(1)}, bf16[8,3,64,1024]{3,2,1,0:T(8,128)(2,1)}, u32[]{:S(2)}) copy-start(bf16[8,3,64,1024]{3,2,1,0:T(8,128)(2,1)} %copy-done) | copy-start | bytes 9437188 | tf_op jit(solution)/shard_map/while
  313.0 42.1 %copy-start.5 = (f32[8]{0:T(128)}, f32[8]{0:T(128)S(1)}, u32[]{:S(2)}) copy-start(f32[8]{0:T(128)S(1)} %get-tuple-element.57) | copy-start | bytes 100
Sparse Core Ops, SparseCore 0:
  108.0 15.0 all-gather.1
where the time goes:
time: 364 us; the launch traced here: 362 us
  blocking collectives  122 us (34%)
  matrix products  113 us (31%)
  local copies, waits for them, and re-layouts  65.8 us (18%)
  other arithmetic  19.6 us (5%)
  between operations  15.5 us (4%)
  waiting for transfers between devices  13 us (4%)
  starting transfers between devices  12.2 us (3%)
    dot_general x8, matrix products, projected_energy(): lax.dot_general(leading, khatri, (((1,), (1,)), ((), ())), preferred_elem...  93.2 us
    all_to_all x1, blocking collectives, body(): lax.all_to_all(coeff_part[asked_rows], 'pair', split_axis=0, concat_axis=...  75.4 us
    unnamed x2, blocking collectives  40.8 us
    dynamic_slice x24, local copies, waits for them, and re-layouts, body(): lax.map(single_triplet, (coeff_trip, paired_trip, tno_coeff, tno_width, i...  17.7 us
    mul x16, local copies, waits for them, and re-layouts, projected_energy(): single_amps[0][None, None, :] * exch_tno[0][:, :, None]  10.9 us
    all_to_all x1, waiting for transfers between devices, body(): lax.all_to_all(paired_part[asked_rows], 'pair', split_axis=0, concat_axis...  10.5 us
    dot_general x8, matrix products, projected_energy(): jnp.einsum('xad,db->xab', pno_coeff, tno_kept, preferred_element_type=jnp...  9.65 us
    dot_general x8, matrix products, projected_energy(): jnp.einsum('xab,xac->xbc', intersection, pno_blocks, preferred_element_ty...  8.29 us
  transfers between devices with their start and end apart: 3, of which 2 were waited for; matrix products, arithmetic and copies ran while one was open for 4% of the time, Pallas kernels for 0%

commit v1 on v0

--- a/solution.py
+++ b/solution.py
@@ -1,46 +1,121 @@
+import functools
+
 import jax
 import jax.numpy as jnp
 from jax import lax
+from jax.experimental import pallas as pl
+from jax.experimental.pallas import tpu as pltpu
 from jax.sharding import PartitionSpec as P
 
-
-def projected_energy(
-    pno_coeff, pno_blocks, tno_block, tno_count, left, right, single_amps, tno_levels, shift
+GROUP = 8
+
+
+def triplet_kernel(
+    pos_ref, width_ref, gap_ref, level_ref, single_ref,
+    c0, c1, c2, p0, p1, p2, tno_ref, left_ref, right_ref, sing_ref, energy_ref,
+    out_ref, lt_ref, at_ref, rm_ref, base_ref, s2_ref, x0_ref, x1_ref, x2_ref, acc_ref,
 ):
-    tno_size = tno_block.shape[1]
-    pno_size = pno_coeff.shape[1]
-    kept_cols = (jnp.arange(tno_size, dtype=jnp.int32) < tno_count).astype(jnp.float32)
-    tno_kept = tno_block * kept_cols.astype(jnp.bfloat16)[None, :]
-    intersection = jnp.einsum(
-        "xad,db->xab", pno_coeff, tno_kept, preferred_element_type=jnp.float32
-    ).astype(jnp.bfloat16)
-    halfway = jnp.einsum(
-        "xab,xac->xbc", intersection, pno_blocks, preferred_element_type=jnp.float32
-    ).astype(jnp.bfloat16)
-    halfway = halfway.reshape(3, tno_size, 2, pno_size)
-    projected = jnp.einsum(
-        "xbkc,xcd->xkbd", halfway, intersection, preferred_element_type=jnp.float32
-    )
-    amps_tno = projected[:, 0].astype(jnp.bfloat16)
-    exch_tno = projected[:, 1]
-    left_cols = jnp.transpose(left, (2, 0, 1)).reshape(tno_size, 3 * tno_size)
-    right_cols = jnp.transpose(right, (2, 0, 1)).reshape(tno_size, 3 * tno_size)
-    khatri = (left_cols[:, None, :] * right_cols[None, :, :]).reshape(
-        tno_size * tno_size, 3 * tno_size
-    )
-    leading = jnp.transpose(amps_tno, (1, 0, 2)).reshape(tno_size, 3 * tno_size)
-    connected = lax.dot_general(
-        leading, khatri, (((1,), (1,)), ((), ())), preferred_element_type=jnp.float32
-    )
-    connected = connected.reshape(tno_size, tno_size, tno_size)
-    complete = connected + single_amps[0][None, None, :] * exch_tno[0][:, :, None]
-    complete = complete + single_amps[1][None, :, None] * exch_tno[1][:, None, :]
-    complete = complete + single_amps[2][:, None, None] * exch_tno[2][None, :, :]
-    denominator = (
-        tno_levels[:, None, None] + tno_levels[None, :, None] + tno_levels[None, None, :] + shift
-    )
-    cube_mask = kept_cols[:, None, None] * kept_cols[None, :, None] * kept_cols[None, None, :]
-    return jnp.sum(cube_mask * connected * complete / denominator)
+    t = pl.program_id(0)
+    width = width_ref[t]
+    pno, tno = c0.shape[1], tno_ref.shape[2]
+    kept = lax.broadcasted_iota(jnp.int32, (1, tno), 1) < width
+    keep = kept.astype(jnp.float32)
+    keep_b = keep.astype(jnp.bfloat16)
+    coeff = jnp.concatenate([c0[0], c1[0], c2[0]], axis=0)
+    inter = jnp.dot(coeff, tno_ref[0], preferred_element_type=jnp.float32)
+    inter = (inter * keep).astype(jnp.bfloat16)
+    for x, blocks in enumerate((p0, p1, p2)):
+        own = inter[x * pno:(x + 1) * pno]
+        half = lax.dot_general(
+            own, blocks[0], (((0,), (0,)), ((), ())), preferred_element_type=jnp.float32
+        ).astype(jnp.bfloat16)
+        amps = jnp.dot(half[:, :pno], own, preferred_element_type=jnp.float32)
+        exch = jnp.dot(half[:, pno:], own, preferred_element_type=jnp.float32)
+        cols = slice(x * tno, (x + 1) * tno)
+        at_ref[:, cols] = amps.astype(jnp.bfloat16)
+        (x0_ref, x1_ref, x2_ref)[x][...] = exch
+        lt_ref[:, cols] = jnp.transpose(left_ref[0, x].astype(jnp.float32) * keep)
+        rm_ref[cols, :] = right_ref[0, x] * keep_b
+    levels = energy_ref[0]
+    base_ref[...] = (
+        jnp.transpose(jnp.broadcast_to(levels, (tno, tno))) + levels + gap_ref[t]
+    )
+    s2_ref[...] = jnp.transpose(jnp.broadcast_to(sing_ref[0, 2:3], (tno, tno)))
+    acc_ref[...] = jnp.zeros_like(acc_ref)
+
+    @pl.loop(0, (width + GROUP - 1) // GROUP)
+    def _(g):
+        first = pl.multiple_of(g * GROUP, GROUP)
+        rows = lt_ref[pl.ds(first, GROUP), :]
+        at = at_ref[...]
+        scaled = [
+            at * jnp.broadcast_to(rows[j:j + 1], at.shape).astype(jnp.bfloat16)
+            for j in range(GROUP)
+        ]
+        conn = jnp.dot(
+            jnp.concatenate(scaled, axis=0), rm_ref[...], preferred_element_type=jnp.float32
+        )
+        x2 = x2_ref[pl.ds(first, GROUP), :]
+        x0 = x0_ref[...]
+        s0 = sing_ref[0, 0:1]
+        total = acc_ref[...]
+        for j in range(GROUP):
+            part = conn[j * tno:(j + 1) * tno]
+            full = part + x0[:, j:j + 1] * s0
+            full = full + single_ref[t, first + j] * x1_ref[...]
+            full = full + s2_ref[...] * x2[j:j + 1]
+            term = part * full / (base_ref[...] + level_ref[t, first + j])
+            total = total + jnp.sum(term.reshape(tno // 8, 8, tno), axis=0)
+        acc_ref[...] = total
+        x0_ref[...] = pltpu.roll(x0, tno - GROUP, 1)
+
+    out_ref[...] = jnp.broadcast_to(jnp.sum(acc_ref[...]), out_ref.shape)
+
+
+def triplet_energies(
+    positions, widths, flat_coeff, flat_paired, tno_coeff, left, right, singles, levels, gap
+):
+    trips, domain, tno = tno_coeff.shape
+    pno = flat_coeff.shape[1]
+
+    def pair_spec(shape, x):
+        return pl.BlockSpec((1,) + shape, lambda t, pos, *_: (pos[t * 3 + x], 0, 0))
+
+    def own_spec(shape):
+        return pl.BlockSpec((1,) + shape, lambda t, *_: (t,) + (0,) * len(shape))
+
+    out = pl.pallas_call(
+        triplet_kernel,
+        out_shape=jax.ShapeDtypeStruct((trips, 1, 128), jnp.float32),
+        grid_spec=pltpu.PrefetchScalarGridSpec(
+            num_scalar_prefetch=5,
+            grid=(trips,),
+            in_specs=[pair_spec((pno, domain), x) for x in range(3)]
+            + [pair_spec((pno, 2 * pno), x) for x in range(3)]
+            + [
+                own_spec((domain, tno)),
+                own_spec((3, tno, tno)),
+                own_spec((3, tno, tno)),
+                own_spec((3, tno)),
+                own_spec((1, tno)),
+            ],
+            out_specs=own_spec((1, 128)),
+            scratch_shapes=[
+                pltpu.VMEM((tno, 3 * tno), jnp.float32),
+                pltpu.VMEM((tno, 3 * tno), jnp.bfloat16),
+                pltpu.VMEM((3 * tno, tno), jnp.bfloat16),
+            ]
+            + [pltpu.VMEM((tno, tno), jnp.float32)] * 5
+            + [pltpu.VMEM((8, tno), jnp.float32)],
+        ),
+        compiler_params=pltpu.CompilerParams(dimension_semantics=("arbitrary",)),
+        name="triplets",
+    )(
+        positions, widths, gap, levels, singles[:, 1],
+        flat_coeff, flat_coeff, flat_coeff, flat_paired, flat_paired, flat_paired,
+        tno_coeff, left, right, singles, levels[:, None, :],
+    )
+    return out[:, 0, 0]
 
 
 def owner_ranks(owners):
@@ -101,26 +176,9 @@
     positions = lax.dynamic_slice_in_dim(positions, replica * ref_count, ref_count)
     flat_coeff = got_coeff.reshape(-1, pno_size, domain)
     flat_paired = got_paired.reshape(-1, pno_size, 2 * pno_size)
-    trips = tno_coeff.shape[0]
-    coeff_trip = flat_coeff[positions].reshape(trips, 3, pno_size, domain)
-    paired_trip = flat_paired[positions].reshape(trips, 3, pno_size, 2 * pno_size)
-
-    def single_triplet(items):
-        return projected_energy(*items)
-
-    energies = lax.map(
-        single_triplet,
-        (
-            coeff_trip,
-            paired_trip,
-            tno_coeff,
-            tno_width,
-            int_left,
-            int_right,
-            singles,
-            tno_energy,
-            gap,
-        ),
+    energies = triplet_energies(
+        positions, tno_width, flat_coeff, flat_paired, tno_coeff, int_left, int_right,
+        singles, tno_energy, gap,
     )
     shares = jnp.repeat(energies / 3.0, 3)
     all_pairs = jnp.arange(owner_count * pair_dev, dtype=jnp.int32)

time: 364 us -> 240 us (0.66)
  matrix products: 113 us -> 0 us
  Pallas kernels: 0 us -> 55.4 us
  local copies, waits for them, and re-layouts: 65.8 us -> 15.3 us
  other arithmetic: 19.6 us -> 7.66 us
    dot_general x32 -> x0, matrix products: 113 us -> none  [the longest x8 93.2 us: projected_energy(): lax.dot_general(leading, khatri, (((1,), (1,)), ((), ())), preferred_elem...]
    pallas_call x0 -> x1, Pallas kernels: none -> 55.4 us  [triplet_energies(): pl.pallas_call(triplet_kernel, out_shape=jax.ShapeDtypeStruct((trips, 1,...]
    mul x48 -> x0, local copies, waits for them, and re-layouts: 19.5 us -> none  [the longest x16 10.9 us: projected_energy(): single_amps[0][None, None, :] * exch_tno[0][:, :, None]]
    dynamic_slice x24 -> x1, local copies, waits for them, and re-layouts: 17.7 us -> 0.58 us  [body(): lax.dynamic_slice_in_dim(positions, replica * ref_count, ref_count)]
    dynamic_update_slice x8 -> x0, local copies, waits for them, and re-layouts: 5.95 us -> none  [body(): lax.map(single_triplet, (coeff_trip, paired_trip, tno_coeff, tno_width, i...]
    mul x8 -> x0, other arithmetic: 5.73 us -> none  [projected_energy(): kept_cols[:, None, None] * kept_cols[None, :, None]]
    add x8 -> x0, local copies, waits for them, and re-layouts: 5.53 us -> none  [projected_energy(): tno_levels[:, None, None] + tno_levels[None, :, None]]
    convert_element_type x8 -> x0, other arithmetic: 5.43 us -> none  [projected_energy(): (jnp.arange(tno_size, dtype=jnp.int32) < tno_count).astype(jnp.float32)]
  transfers between devices with their start and end apart: 3 -> 3, of which waited for: 2 -> 2; matrix products, arithmetic and copies ran while one was open for 4% -> 6% of each run, Pallas kernels for 0% -> 0%
where the time goes in v1:
time: 240 us
  blocking collectives  122 us (51%)
  Pallas kernels  55.4 us (23%)
  between operations  15.5 us (6%)
  local copies, waits for them, and re-layouts  15.3 us (6%)
  starting transfers between devices  12.2 us (5%)
  waiting for transfers between devices  11.4 us (5%)
  other arithmetic  7.66 us (3%)
    all_to_all x1, blocking collectives, body(): lax.all_to_all(coeff_part[asked_rows], 'pair', split_axis=0, concat_axis=...  75.3 us
    pallas_call x1, Pallas kernels, triplet_energies(): pl.pallas_call(triplet_kernel, out_shape=jax.ShapeDtypeStruct((trips, 1,...  55.4 us
    unnamed x2, blocking collectives  41.2 us
    all_to_all x1, waiting for transfers between devices, body(): lax.all_to_all(paired_part[asked_rows], 'pair', split_axis=0, concat_axis...  8.83 us
    all_to_all x1, starting transfers between devices, body(): lax.all_to_all(requests, 'pair', split_axis=0, concat_axis=0, tiled=True)  8.19 us
    unnamed x15, local copies, waits for them, and re-layouts  5.3 us
  transfers between devices with their start and end apart: 3, of which 2 were waited for; matrix products, arithmetic and copies ran while one was open for 6% of the time, Pallas kernels for 0%

profile of v1, /device:TPU:0, one launch (start us, length us, event | category | flops | bytes accessed | tf_op | source)
XLA Modules:
  0.0 239.8 jit_solution(17555583016789326716)
XLA Ops:
  7.2 0.8 copy.35
  8.0 1.2 dynamic-slice
  9.9 0.2 dynamic-update-slice
  10.2 2.0 all-reduce
  12.1 0.2 convert_reduce_fusion
  12.3 0.7 scatter_custom_fusion
  13.1 0.7 all_to_all.14
  13.7 8.2 %all-to-all-start = ((s32[16,1,3]{2,1,0:T(1,128)}), s32[16,1,3]{2,1,0:T(1,128)S(1)}, u32[]{:S(2)}, u32[]{:S(2)}) async-start(s32[16,1,3]{2,1,0:T(1,128)} %bitcast.2), calls=%async_computation | async-start | bytes 16384 | tf_op jit(solution)/shard_map/all_to_all | solution.py:163
  22.0 0.7 fusion
  22.7 4.0 %dynamic-slice_multiply_fusion = bf16[64,64,512]{2,1,0:T(8,128)(2,1)} fusion(bf16[64,64,1024]{2,1,0:T(8,128)(2,1)} %param.15, s32[]{:T(128)S(6)} %select_n.41, bf16[64,64]{1,0:T(8,128)(2,1)S(1)} %fusion), kind=kLoop, calls=%fused_computation.3 | loop fusion | flops 8388608 | bytes 8396804 | tf_op jit(solution)/shard_map/mul | solution.py:152
  26.7 2.5 %all-to-all-done = s32[16,1,3]{2,1,0:T(1,128)S(1)} async-done(((s32[16,1,3]{2,1,0:T(1,128)}), s32[16,1,3]{2,1,0:T(1,128)S(1)}, u32[]{:S(2)}, u32[]{:S(2)}) %all-to-all-start) | async-done | bytes 224 | tf_op jit(solution)/shard_map/all_to_all | solution.py:163
  29.4 0.1 reshape.76
  29.5 2.9 %gather_fusion = bf16[48,64,512]{2,1,0:T(8,128)(2,1)S(1)} fusion(bf16[64,64,512]{2,1,0:T(8,128)(2,1)} %dynamic-slice_multiply_fusion, s32[1024]{0:T(1024)S(1)} %pad_clamp_fusion), kind=kCustom, calls=%fused_computation | custom fusion | bytes 6291648 | tf_op jit(solution)/shard_map/gather | solution.py:168
  32.5 75.3 %all_to_all.22 = bf16[16,3,64,512]{3,2,1,0:T(8,128)(2,1)} all-to-all(bf16[16,3,64,512]{3,2,1,0:T(8,128)(2,1)S(1)} %bitcast.20), channel_id=1, replica_groups=mesh['pair'=16,'rep'=2] {'pair'}, dimensions={0} | all-to-all | bytes 6291456 | tf_op jit(solution)/shard_map/all_to_all | solution.py:168
  107.8 2.6 %dynamic-slice_maximum_fusion = bf16[64,64,64]{2,1,0:T(8,128)(2,1)S(1)} fusion(s32[]{:T(128)S(6)} %select_n.45, bf16[64,64,64]{2,1,0:T(8,128)(2,1)} %param.17, bf16[64,64,64]{2,1,0:T(8,128)(2,1)} %param.16), kind=kLoop, calls=%fused_computation.4 | loop fusion | flops 1048576 | bytes 1572868 | tf_op jit(solution)/shard_map/concatenate | solution.py:153
  110.4 0.7 gather_fusion.1
  111.2 1.3 reshape.110
  112.4 3.9 %all-to-all-start.2 = ((bf16[16,2,6144]{2,1,0:T(2,128)(2,1)}), bf16[16,2,6144]{2,1,0:T(2,128)(2,1)S(1)}, u32[]{:S(2)}, u32[]{:S(2)}) async-start(bf16[16,2,6144]{2,1,0:T(2,128)(2,1)} %reshape.110), calls=%async_computation.2 | async-start | bytes 786432 | tf_op jit(solution)/shard_map/all_to_all | solution.py:169
  116.4 0.6 copy.41.sing_ref
  117.0 0.6 dynamic_slice.9.pos_ref
  117.6 0.6 dynamic-slice.1
  118.9 0.6 slice_bitcast_fusion.single_ref
  119.4 8.8 %all-to-all-done.2 = bf16[16,2,6144]{2,1,0:T(2,128)(2,1)S(1)} async-done(((bf16[16,2,6144]{2,1,0:T(2,128)(2,1)}), bf16[16,2,6144]{2,1,0:T(2,128)(2,1)S(1)}, u32[]{:S(2)}, u32[]{:S(2)}) %all-to-all-start.2) | async-done | bytes 393248 | tf_op jit(solution)/shard_map/all_to_all | solution.py:169
  128.3 0.5 reshape.111
  128.8 0.6 copy.39
  129.4 2.9 %all_gather.11 = bf16[16,3,64,128]{2,0,1,3:T(8,128)(2,1)S(1)} all-gather(bf16[16,3,64,64]{2,0,1,3:T(8,128)(2,1)S(1)} %copy.39), channel_id=1, replica_groups=mesh['pair'=16,'rep'=2] {'rep'}, dimensions={3}, use_global_device_ids=true | all-gather | bytes 1179648 | tf_op jit(solution)/shard_map/all_gather | solution.py:173
  132.3 1.9 copy.40
  134.2 55.4 %triplets.1 = f32[8,1,128]{2,1,0:T(1,128)} custom-call(s32[24]{0:T(128)} %dynamic_slice.9.pos_ref, s32[8]{0:T(128)} %width_ref.1, f32[8]{0:T(128)} %gap_ref.1, f32[8,128]{1,0:T(8,128)} %level_ref.1, f32[8,128]{1,0:T(8,128)} %slice_bitcast_fusion.single_ref, bf16[48,64,1024]{2,1,0:T(8,128)(2,1)} %bitcast.14, bf16[48,64,1024]{2,1,0:T(8,128)(2,1)} %bitcast.15, ...), custom_call_target="tpu_custom_call" | custom-call | tf_op jit(solution)/shard_map/triplets/pallas_call | solution.py:87
  189.6 0.8 slice_reduce_fusion
  190.6 0.1 select_reduce_fusion
  190.7 39.3 %all-reduce.1 = f32[1024]{0:T(1024)S(1)} all-reduce(f32[1024]{0:T(1024)S(1)} %select_reduce_fusion), channel_id=2, replica_groups=mesh['pair'=16,'rep'=2] {'pair'}, use_global_device_ids=true, to_apply=%region_3.4.clone | all-reduce | flops 1024 | bytes 8192
  230.0 2.9 %psum.7 = f32[64]{0:T(128)} all-reduce(f32[64]{0:T(128)S(1)} %dynamic-slice.2), channel_id=1, replica_groups=mesh['pair'=16,'rep'=2] {'rep'}, use_global_device_ids=true, to_apply=%region_4.5 | all-reduce | flops 64 | bytes 512 | tf_op jit(solution)/shard_map/psum | solution.py:189
  (21 shorter events, 0.6 us)
Async XLA Ops:
  13.7 15.5 %all-to-all-start = ((s32[16,1,3]{2,1,0:T(1,128)}), s32[16,1,3]{2,1,0:T(1,128)S(1)}, u32[]{:S(2)}, u32[]{:S(2)}) async-start(s32[16,1,3]{2,1,0:T(1,128)} %bitcast.2), calls=%async_computation | async-start | bytes 16384 | tf_op jit(solution)/shard_map/all_to_all | solution.py:163
  21.9 112.3 %all-gather.2.cloned.1.call-start = ((), (), s32[]{:S(2)}) async-start(), calls=%async_computation.3 | async-start | bytes 9437184 | tf_op jit(solution)/shard_map/all_gather | solution.py:172
  107.8 8.6 %copy-start = (f32[8,3,128]{2,0,1:T(8,128)S(1)}, f32[8,3,128]{2,0,1:T(8,128)}, u32[]{:S(2)}) copy-start(f32[8,3,128]{2,0,1:T(8,128)} %param.21) | copy-start | bytes 36868
  107.8 9.8 %copy-start.2 = (u32[32]{0:T(128)S(1)}, u32[32]{0:T(128)}, u32[]{:S(2)}) copy-start(u32[32]{0:T(128)} %constant.70) | copy-start | bytes 388
  112.4 15.8 %all-to-all-start.2 = ((bf16[16,2,6144]{2,1,0:T(2,128)(2,1)}), bf16[16,2,6144]{2,1,0:T(2,128)(2,1)S(1)}, u32[]{:S(2)}, u32[]{:S(2)}) async-start(bf16[16,2,6144]{2,1,0:T(2,128)(2,1)} %reshape.110), calls=%async_computation.2 | async-start | bytes 786432 | tf_op jit(solution)/shard_map/all_to_all | solution.py:169
  190.4 42.5 %copy-start.1 = (f32[8]{0:T(128)}, f32[8]{0:T(128)S(1)}, u32[]{:S(2)}) copy-start(f32[8]{0:T(128)S(1)} %slice_reduce_fusion) | copy-start | bytes 100
Sparse Core Ops, SparseCore 0:
  108.0 15.0 all-gather.1

commit v2 on v1

--- a/solution.py
+++ b/solution.py
@@ -17,17 +17,31 @@
 ):
     t = pl.program_id(0)
     width = width_ref[t]
-    pno, tno = c0.shape[1], tno_ref.shape[2]
+    pno, tno = c0.shape[2], tno_ref.shape[2]
+    half_dom = c0.shape[3]
     kept = lax.broadcasted_iota(jnp.int32, (1, tno), 1) < width
     keep = kept.astype(jnp.float32)
     keep_b = keep.astype(jnp.bfloat16)
-    coeff = jnp.concatenate([c0[0], c1[0], c2[0]], axis=0)
-    inter = jnp.dot(coeff, tno_ref[0], preferred_element_type=jnp.float32)
+    inter = sum(
+        jnp.dot(
+            jnp.concatenate([c0[h, 0], c1[h, 0], c2[h, 0]], axis=0),
+            tno_ref[0, h * half_dom:(h + 1) * half_dom],
+            preferred_element_type=jnp.float32,
+        )
+        for h in range(2)
+    )
     inter = (inter * keep).astype(jnp.bfloat16)
     for x, blocks in enumerate((p0, p1, p2)):
         own = inter[x * pno:(x + 1) * pno]
+        pair = jnp.concatenate(
+            [
+                jnp.concatenate([blocks[h, 0, :, :pno], blocks[h, 0, :, pno:]], axis=0)
+                for h in range(2)
+            ],
+            axis=1,
+        )
         half = lax.dot_general(
-            own, blocks[0], (((0,), (0,)), ((), ())), preferred_element_type=jnp.float32
+            own, pair, (((0,), (0,)), ((), ())), preferred_element_type=jnp.float32
         ).astype(jnp.bfloat16)
         amps = jnp.dot(half[:, :pno], own, preferred_element_type=jnp.float32)
         exch = jnp.dot(half[:, pno:], own, preferred_element_type=jnp.float32)
@@ -76,10 +90,10 @@
     positions, widths, flat_coeff, flat_paired, tno_coeff, left, right, singles, levels, gap
 ):
     trips, domain, tno = tno_coeff.shape
-    pno = flat_coeff.shape[1]
+    pno = flat_coeff.shape[2]
 
     def pair_spec(shape, x):
-        return pl.BlockSpec((1,) + shape, lambda t, pos, *_: (pos[t * 3 + x], 0, 0))
+        return pl.BlockSpec((2, 1) + shape, lambda t, pos, *_: (0, pos[t * 3 + x], 0, 0))
 
     def own_spec(shape):
         return pl.BlockSpec((1,) + shape, lambda t, *_: (t,) + (0,) * len(shape))
@@ -90,8 +104,8 @@
         grid_spec=pltpu.PrefetchScalarGridSpec(
             num_scalar_prefetch=5,
             grid=(trips,),
-            in_specs=[pair_spec((pno, domain), x) for x in range(3)]
-            + [pair_spec((pno, 2 * pno), x) for x in range(3)]
+            in_specs=[pair_spec((pno, domain // 2), x) for x in range(3)]
+            + [pair_spec((pno // 2, 2 * pno), x) for x in range(3)]
             + [
                 own_spec((domain, tno)),
                 own_spec((3, tno, tno)),
@@ -115,14 +129,208 @@
         flat_coeff, flat_coeff, flat_coeff, flat_paired, flat_paired, flat_paired,
         tno_coeff, left, right, singles, levels[:, None, :],
     )
-    return out[:, 0, 0]
-
-
-def owner_ranks(owners):
-    matching = owners[:, None] == owners[None, :]
-    position = jnp.arange(owners.shape[0], dtype=jnp.int32)
-    earlier = position[None, :] < position[:, None]
-    return jnp.sum(jnp.logical_and(matching, earlier), axis=1)
+    return out[:, 0]
+
+
+MESH = pl.DeviceIdType.MESH
+
+
+def share_kernel(count, reps, x_ref, out_ref, send_sem, recv_sem):
+    me = lax.axis_index("pair") * reps + lax.axis_index("rep")
+    barrier = pltpu.get_barrier_semaphore()
+
+    @pl.loop(1, count)
+    def _(d):
+        other = lax.rem(me + d, count)
+        pl.semaphore_signal(
+            barrier, inc=1, device_id=(other // reps, lax.rem(other, reps)), device_id_type=MESH
+        )
+
+    pl.semaphore_wait(barrier, count - 1)
+
+    def copy(d):
+        other = lax.rem(me + d, count)
+        return pltpu.make_async_remote_copy(
+            src_ref=x_ref,
+            dst_ref=out_ref.at[me],
+            send_sem=send_sem.at[d - 1],
+            recv_sem=recv_sem.at[d - 1],
+            device_id=(other // reps, lax.rem(other, reps)),
+            device_id_type=MESH,
+        )
+
+    @pl.loop(1, count)
+    def _(d):
+        copy(d).start()
+
+    out_ref[me] = x_ref[...]
+
+    @pl.loop(1, count)
+    def _(d):
+        copy(d).wait()
+
+
+def share(block, cid):
+    owners, reps = lax.axis_size("pair"), lax.axis_size("rep")
+    count = owners * reps
+    return pl.pallas_call(
+        functools.partial(share_kernel, count, reps),
+        out_shape=jax.ShapeDtypeStruct((count,) + block.shape, block.dtype),
+        in_specs=[pl.BlockSpec(memory_space=pltpu.VMEM)],
+        out_specs=pl.BlockSpec(memory_space=pltpu.VMEM),
+        scratch_shapes=[
+            pltpu.SemaphoreType.DMA((count - 1,)),
+            pltpu.SemaphoreType.DMA((count - 1,)),
+        ],
+        compiler_params=pltpu.CompilerParams(collective_id=cid, has_side_effects=True),
+        name="share" + str(cid),
+    )(block)
+
+
+def exchange_kernel(
+    count, coeff_ref, block_ref, got_coeff, got_block,
+    keep_coeff, keep_block, send_sem, recv_sem, pass_sem, land_sem, local_sem,
+):
+    me, rep = lax.axis_index("pair"), lax.axis_index("rep")
+    sibling = (me, 1 - rep)
+    barrier = pltpu.get_barrier_semaphore()
+    pl.semaphore_signal(barrier, inc=1, device_id=sibling, device_id_type=MESH)
+
+    @pl.loop(1, count)
+    def _(d):
+        pl.semaphore_signal(
+            barrier, inc=1, device_id=(lax.rem(me + d, count), rep), device_id_type=MESH
+        )
+
+    pl.semaphore_wait(barrier, count)
+
+    def send(d, k):
+        other = lax.rem(me + d, count)
+        return pltpu.make_async_remote_copy(
+            src_ref=(coeff_ref, block_ref)[k].at[other],
+            dst_ref=(got_coeff, got_block)[k].at[rep, me],
+            send_sem=send_sem.at[k, d - 1],
+            recv_sem=recv_sem.at[k, d - 1],
+            device_id=(other, rep),
+            device_id_type=MESH,
+        )
+
+    def forward(d, k):
+        origin = lax.rem(me - d + count, count)
+        return pltpu.make_async_remote_copy(
+            src_ref=(got_coeff, got_block)[k].at[rep, origin],
+            dst_ref=(got_coeff, got_block)[k].at[rep, origin],
+            send_sem=pass_sem.at[k, d],
+            recv_sem=land_sem.at[k, d],
+            device_id=sibling,
+            device_id_type=MESH,
+        )
+
+    far_first = sorted(range(1, count), key=lambda d: (-min(d, count - d), d))
+    for d in far_first:
+        for k in (1, 0):
+            send(d, k).start()
+
+    own = []
+    for k in range(2):
+        source, held = (coeff_ref, block_ref)[k], (keep_coeff, keep_block)[k]
+        target = (got_coeff, got_block)[k]
+        own.append((
+            pltpu.make_async_copy(source.at[me], held, local_sem.at[k, 0]),
+            pltpu.make_async_copy(held, target.at[rep, me], local_sem.at[k, 1]),
+        ))
+    for load, _ in own:
+        load.start()
+    for load, store in own:
+        load.wait()
+        store.start()
+    for _, store in own:
+        store.wait()
+    for k in range(2):
+        forward(0, k).start()
+    for d in far_first[::-1]:
+        for k in (1, 0):
+            send(d, k).wait_recv()
+            forward(d, k).start()
+
+    @pl.loop(1, count)
+    def _(d):
+        for k in range(2):
+            send(d, k).wait_send()
+
+    @pl.loop(0, count)
+    def _(d):
+        for k in range(2):
+            forward(d, k).wait()
+
+
+def exchange(coeff, block, cid):
+    count = coeff.shape[0]
+    shapes = [jax.ShapeDtypeStruct((2,) + a.shape, a.dtype) for a in (coeff, block)]
+    return pl.pallas_call(
+        functools.partial(exchange_kernel, count),
+        out_shape=shapes,
+        in_specs=[pl.BlockSpec(memory_space=pl.ANY)] * 2,
+        out_specs=[pl.BlockSpec(memory_space=pl.ANY)] * 2,
+        scratch_shapes=[
+            pltpu.VMEM(coeff.shape[1:], coeff.dtype),
+            pltpu.VMEM(block.shape[1:], block.dtype),
+            pltpu.SemaphoreType.DMA((2, count - 1)),
+            pltpu.SemaphoreType.DMA((2, count - 1)),
+            pltpu.SemaphoreType.DMA((2, count)),
+            pltpu.SemaphoreType.DMA((2, count)),
+            pltpu.SemaphoreType.DMA((2, 2)),
+        ],
+        compiler_params=pltpu.CompilerParams(collective_id=cid, has_side_effects=True),
+        name="exchange",
+    )(coeff, block)
+
+
+def gather_kernel(row_ref, rep_ref, coeff_ref, out_ref, held, in_sem, out_sem):
+    total, _, half = held.shape
+    start = pl.multiple_of(rep_ref[0] * half, half)
+
+    def load(i):
+        return pltpu.make_async_copy(
+            coeff_ref.at[row_ref[i], :, pl.ds(start, half)], held.at[i], in_sem.at[i]
+        )
+
+    def store(i):
+        return pltpu.make_async_copy(held.at[i], out_ref.at[i], out_sem.at[i])
+
+    @pl.loop(0, total)
+    def _(i):
+        load(i).start()
+
+    @pl.loop(0, total)
+    def _(i):
+        load(i).wait()
+        store(i).start()
+
+    @pl.loop(0, total)
+    def _(i):
+        store(i).wait()
+
+
+def gather_rows(coeff, rows, rep):
+    _, pno, domain = coeff.shape
+    total = rows.shape[0]
+    return pl.pallas_call(
+        gather_kernel,
+        out_shape=jax.ShapeDtypeStruct((total, pno, domain // 2), coeff.dtype),
+        grid_spec=pltpu.PrefetchScalarGridSpec(
+            num_scalar_prefetch=2,
+            grid=(),
+            in_specs=[pl.BlockSpec(memory_space=pl.ANY)],
+            out_specs=pl.BlockSpec(memory_space=pl.ANY),
+            scratch_shapes=[
+                pltpu.VMEM((total, pno, domain // 2), coeff.dtype),
+                pltpu.SemaphoreType.DMA((total,)),
+                pltpu.SemaphoreType.DMA((total,)),
+            ],
+        ),
+        name="gather_rows",
+    )(rows, rep.reshape(1), coeff)
 
 
 def body(
@@ -140,54 +348,51 @@
     gap,
 ):
     owner_count = lax.axis_size("pair")
-    pair_dev = pair_coeff.shape[0]
-    pno_size = pair_coeff.shape[1]
-    domain = pair_coeff.shape[2]
-    references = triplet_pairs.reshape(-1)
-    ref_count = references.shape[0]
+    replica, me = lax.axis_index("rep"), lax.axis_index("pair")
+    pair_dev, pno, domain = pair_coeff.shape
+    trips, tno = tno_coeff.shape[0], tno_coeff.shape[2]
+    ref_count = 3 * trips
     capacity = (2 * ref_count + owner_count - 1) // owner_count
-    kept_rows = (jnp.arange(pno_size, dtype=jnp.int32)[None, :] < pair_width[:, None]).astype(
-        jnp.bfloat16
-    )
-    masked = pair_coeff * kept_rows[:, :, None]
-    paired = jnp.concatenate([pair_amps, pair_exch], axis=2)
-    chip_refs = lax.all_gather(references, "rep", axis=0, tiled=True)
+
+    padded = jnp.pad(triplet_pairs, ((0, 0), (0, 128 - 3)))
+    shared = share(padded, 0)[:, :, :3]
+    ids = shared.reshape(owner_count, 2 * ref_count)
+    mine = (ids // pair_dev == me).astype(jnp.float32)
+    spot = jnp.arange(2 * ref_count, dtype=jnp.int32)
+    before = (spot[:, None] < spot[None, :]).astype(jnp.float32)
+    rank = jnp.dot(mine, before)
+    slots = jnp.arange(capacity, dtype=jnp.int32).astype(jnp.float32)
+    chosen = (mine[:, None, :] > 0) & (rank[:, None, :] == slots[None, :, None])
+    rows = jnp.sum(jnp.where(chosen, (ids % pair_dev)[:, None, :], 0), axis=2).reshape(-1)
+
+    inside = jnp.arange(pno, dtype=jnp.int32)[None, :] < pair_width[:, None]
+    square = inside[:, :, None] & inside[:, None, :]
+    block = jnp.where(square, jnp.where(replica == 0, pair_amps, pair_exch), 0)
+    block = jnp.concatenate([block[:, :pno // 2], block[:, pno // 2:]], axis=2)
+    send_block = block[rows].reshape(owner_count, capacity, pno // 2, 2 * pno)
+    send_coeff = gather_rows(pair_coeff, rows, replica)
+    send_coeff = send_coeff.reshape(owner_count, capacity, pno, domain // 2)
+    got_coeff, got_block = exchange(send_coeff, send_block, 1)
+
+    chip_refs = lax.dynamic_index_in_dim(ids, me, 0, keepdims=False)
     owners = chip_refs // pair_dev
-    slot_rank = owner_ranks(owners)
-    requests = (
-        jnp.zeros((owner_count * capacity,), jnp.int32)
-        .at[owners * capacity + slot_rank]
-        .set(chip_refs % pair_dev)
-    )
-    requests = requests.reshape(owner_count, capacity)
-    asked_rows = lax.all_to_all(requests, "pair", split_axis=0, concat_axis=0, tiled=True)
-    replica = lax.axis_index("rep")
-    coeff_part = lax.dynamic_slice_in_dim(masked, replica * (domain // 2), domain // 2, 2)
-    paired_part = lax.dynamic_slice_in_dim(paired, replica * pno_size, pno_size, 2)
-    got_coeff, got_paired = (
-        lax.all_to_all(coeff_part[asked_rows], "pair", split_axis=0, concat_axis=0, tiled=True),
-        lax.all_to_all(paired_part[asked_rows], "pair", split_axis=0, concat_axis=0, tiled=True),
-    )
-    got_coeff, got_paired = (
-        lax.all_gather(got_coeff, "rep", axis=3, tiled=True),
-        lax.all_gather(got_paired, "rep", axis=3, tiled=True),
-    )
-    positions = owners * capacity + slot_rank
+    earlier = (owners[:, None] == owners[None, :]) & (spot[None, :] < spot[:, None])
+    positions = owners * capacity + jnp.sum(earlier.astype(jnp.int32), axis=1)
     positions = lax.dynamic_slice_in_dim(positions, replica * ref_count, ref_count)
-    flat_coeff = got_coeff.reshape(-1, pno_size, domain)
-    flat_paired = got_paired.reshape(-1, pno_size, 2 * pno_size)
     energies = triplet_energies(
-        positions, tno_width, flat_coeff, flat_paired, tno_coeff, int_left, int_right,
-        singles, tno_energy, gap,
-    )
-    shares = jnp.repeat(energies / 3.0, 3)
-    all_pairs = jnp.arange(owner_count * pair_dev, dtype=jnp.int32)
-    dense = jnp.sum(
-        jnp.where(references[:, None] == all_pairs[None, :], shares[:, None], 0.0), axis=0
-    )
-    owned = lax.psum_scatter(dense, "pair", scatter_dimension=0, tiled=True)
-    pair_energy = lax.psum(owned, "rep")
-    return (energies, pair_energy)
+        positions,
+        tno_width,
+        got_coeff.reshape(2, -1, pno, domain // 2),
+        got_block.reshape(2, -1, pno // 2, 2 * pno),
+        tno_coeff, int_left, int_right, singles, tno_energy, gap,
+    )
+    everyone = share(energies, 2)[:, :, 0].reshape(-1)
+    owned = jnp.arange(pair_dev, dtype=jnp.int32) + me * pair_dev
+    shares = jnp.repeat(everyone / 3.0, 3)
+    pair_energy = jnp.sum(
+        jnp.where(ids.reshape(-1)[None, :] == owned[:, None], shares[None, :], 0.0), axis=1
+    )
+    return (energies[:, 0], pair_energy)
 
 
 def solution(mesh):

time: 240 us -> 199 us (0.83)
  Pallas kernels: 55.4 us -> 182 us
  blocking collectives: 122 us -> 0 us
  between operations: 15.5 us -> 0.78 us
  starting transfers between devices: 12.2 us -> 0 us
  waiting for transfers between devices: 11.4 us -> 0 us
  local copies, waits for them, and re-layouts: 15.3 us -> 10.6 us
    pallas_call x0 -> x4, Pallas kernels: none -> 128 us  [the longest x1 80.1 us: exchange(): pl.pallas_call(functools.partial(exchange_kernel, count), out_shape=shape...]
    all_to_all x1 -> x0, blocking collectives: 75.3 us -> none  [body(): lax.all_to_all(coeff_part[asked_rows], 'pair', split_axis=0, concat_axis=...]
    unnamed x2 -> x0, blocking collectives: 41.2 us -> none
    all_to_all x2 -> x0, starting transfers between devices: 12.1 us -> none  [the longest x1 8.19 us: body(): lax.all_to_all(requests, 'pair', split_axis=0, concat_axis=0, tiled=True)]
    all_to_all x2 -> x0, waiting for transfers between devices: 11.3 us -> none  [the longest x1 8.83 us: body(): lax.all_to_all(paired_part[asked_rows], 'pair', split_axis=0, concat_axis...]
    mul x1 -> x0, other arithmetic: 4.02 us -> none  [body(): masked = pair_coeff * kept_rows[:, :, None]]
    unnamed x15 -> x2, local copies, waits for them, and re-layouts: 5.3 us -> 2.07 us
    psum x1 -> x0, blocking collectives: 2.95 us -> none  [body(): pair_energy = lax.psum(owned, 'rep')]
  transfers between devices with their start and end apart: 3 -> 0, of which waited for: 2 -> 0; matrix products, arithmetic and copies ran while one was open for 6% -> 0% of each run, Pallas kernels for 0% -> 0%
where the time goes in v2:
time: 199 us
  Pallas kernels  182 us (91%)
  local copies, waits for them, and re-layouts  10.6 us (5%)
  other arithmetic  5.85 us (3%)
    pallas_call x1, Pallas kernels, exchange(): pl.pallas_call(functools.partial(exchange_kernel, count), out_shape=shape...  80.1 us
    pallas_call x1, Pallas kernels, triplet_energies(): pl.pallas_call(triplet_kernel, out_shape=jax.ShapeDtypeStruct((trips, 1,...  53.7 us
    pallas_call x2, Pallas kernels, share(): pl.pallas_call(functools.partial(share_kernel, count, reps), out_shape=ja...  43.5 us
    pallas_call x1, Pallas kernels, gather_rows(): pl.pallas_call(gather_kernel, out_shape=jax.ShapeDtypeStruct((total, pno,...  4.5 us

profile of v2, /device:TPU:0, one launch (start us, length us, event | category | flops | bytes accessed | tf_op | source)
XLA Modules:
  0.0 199.2 jit_solution(3018077660771957566)
XLA Ops:
  0.7 0.8 copy.18
  1.4 0.6 pad.4.x_ref
  2.0 1.3 slice_bitcast_fusion.single_ref
  3.3 0.7 iota_compare_fusion
  4.0 1.3 copy.21.sing_ref
  5.3 11.9 %share0.1 = s32[32,8,128]{2,1,0:T(8,128)} custom-call(s32[8,128]{1,0:T(8,128)} %pad.4.x_ref), custom_call_target="tpu_custom_call" | custom-call | tf_op jit(solution)/shard_map/share0/pallas_call | solution.py:176
  17.3 1.1 eq.68
  18.4 1.0 reshape.185
  19.4 0.2 convert_reduce_fusion
  19.6 0.6 dynamic_slice.8.pos_ref
  20.2 0.1 fusion.1
  20.4 0.2 select_reduce_fusion.1
  20.6 0.1 copy.19
  20.7 0.1 reshape.189
  20.8 0.7 reshape.186.row_ref
  21.4 2.6 %and_select_fusion = bf16[64,64,64]{2,1,0:T(8,128)(2,1)S(1)} fusion(bf16[64,64,64]{2,1,0:T(8,128)(2,1)} %param.16, bf16[64,64,64]{2,1,0:T(8,128)(2,1)} %param.17, pred[]{:T(512)S(6)} %eq.67, pred[64,64]{1,0:T(8,128)(4,1)S(1)} %iota_compare_fusion), kind=kLoop, calls=%fused_computation.1 | loop fusion | flops 786432 | bytes 1576961 | tf_op jit(solution)/shard_map/jit(_where)/select_n | solution.py:370
  24.1 0.1 fusion.8
  24.2 0.3 pad_maximum_fusion
  24.5 1.3 gather_fusion
  25.8 4.5 %gather_rows.1 = bf16[48,64,512]{2,1,0:T(8,128)(2,1)} custom-call(s32[48]{0:T(128)} %reshape.186.row_ref, s32[1]{0:T(128)} %bitcast.3.rep_ref, bf16[64,64,1024]{2,1,0:T(8,128)(2,1)} %coeff_ref.1), custom_call_target="tpu_custom_call" | custom-call | tf_op jit(solution)/shard_map/gather_rows/pallas_call | solution.py:318
  30.3 80.1 %exchange.1 = (bf16[2,16,3,64,512]{4,3,2,1,0:T(8,128)(2,1)}, bf16[2,16,3,32,128]{4,3,2,1,0:T(8,128)(2,1)}) custom-call(bf16[16,3,64,512]{3,2,1,0:T(8,128)(2,1)} %bitcast.28, bf16[16,3,32,128]{3,2,1,0:T(8,128)(2,1)} %bitcast.32), custom_call_target="tpu_custom_call" | custom-call | tf_op jit(solution)/shard_map/exchange/pallas_call | solution.py:270
  110.4 53.7 %triplets.1 = f32[8,1,128]{2,1,0:T(1,128)} custom-call(s32[24]{0:T(128)} %dynamic_slice.8.pos_ref, s32[8]{0:T(128)} %width_ref.1, f32[8]{0:T(128)} %gap_ref.1, f32[8,128]{1,0:T(8,128)} %level_ref.1, f32[8,128]{1,0:T(8,128)} %slice_bitcast_fusion.single_ref, bf16[2,48,64,512]{3,2,1,0:T(8,128)(2,1)} %bitcast.25, bf16[2,48,64,512]{3,2,1,0:T(8,128)(2,1)} %bitcast.26, ...), custom_call_target="tpu_custom_call" | custom-call | tf_op jit(solution)/shard_map/triplets/pallas_call | solution.py:101
  164.1 1.3 slice_reduce_fusion
  165.4 31.6 %share2.1 = f32[32,8,128]{2,1,0:T(8,128)} custom-call(f32[8,128]{1,0:T(8,128)} %bitcast.36), custom_call_target="tpu_custom_call" | custom-call | tf_op jit(solution)/shard_map/share2/pallas_call | solution.py:176
  197.0 1.0 multiply_reduce_fusion
  198.1 0.1 div.54
  198.2 0.1 broadcast_in_dim.56
  198.3 0.2 broadcast_in_dim.57
  198.5 0.7 select_reduce_fusion
  (9 shorter events, 0.1 us)

commit v3 on v2

--- a/solution.py
+++ b/solution.py
@@ -8,6 +8,7 @@
 from jax.sharding import PartitionSpec as P
 
 GROUP = 8
+ROW_STEP = 16
 
 
 def triplet_kernel(
@@ -57,11 +58,37 @@
     s2_ref[...] = jnp.transpose(jnp.broadcast_to(sing_ref[0, 2:3], (tno, tno)))
     acc_ref[...] = jnp.zeros_like(acc_ref)
 
+    for low in range(tno // 2, tno + 1, ROW_STEP):
+        fits = width <= low
+        if low > tno // 2:
+            fits = fits & (width > low - ROW_STEP)
+
+        @pl.when(fits)
+        def _(low=low):
+            contract(
+                low, t, width, level_ref, single_ref, sing_ref, lt_ref, at_ref, rm_ref,
+                base_ref, s2_ref, x0_ref, x1_ref, x2_ref, acc_ref,
+            )
+
+    @pl.when(t == 0)
+    def _():
+        out_ref[...] = jnp.zeros_like(out_ref)
+
+    here = lax.broadcasted_iota(jnp.int32, out_ref.shape, 1) == t
+    out_ref[...] = jnp.where(here, jnp.sum(acc_ref[...]), out_ref[...])
+
+
+def contract(
+    low, t, width, level_ref, single_ref, sing_ref, lt_ref, at_ref, rm_ref,
+    base_ref, s2_ref, x0_ref, x1_ref, x2_ref, acc_ref,
+):
+    tno = rm_ref.shape[1]
+
     @pl.loop(0, (width + GROUP - 1) // GROUP)
     def _(g):
         first = pl.multiple_of(g * GROUP, GROUP)
         rows = lt_ref[pl.ds(first, GROUP), :]
-        at = at_ref[...]
+        at = at_ref[:low]
         scaled = [
             at * jnp.broadcast_to(rows[j:j + 1], at.shape).astype(jnp.bfloat16)
             for j in range(GROUP)
@@ -70,20 +97,28 @@
             jnp.concatenate(scaled, axis=0), rm_ref[...], preferred_element_type=jnp.float32
         )
         x2 = x2_ref[pl.ds(first, GROUP), :]
-        x0 = x0_ref[...]
+        x0 = x0_ref[:low]
         s0 = sing_ref[0, 0:1]
         total = acc_ref[...]
-        for j in range(GROUP):
-            part = conn[j * tno:(j + 1) * tno]
+
+        def pieces(j):
+            part = conn[j * low:(j + 1) * low]
             full = part + x0[:, j:j + 1] * s0
-            full = full + single_ref[t, first + j] * x1_ref[...]
-            full = full + s2_ref[...] * x2[j:j + 1]
-            term = part * full / (base_ref[...] + level_ref[t, first + j])
-            total = total + jnp.sum(term.reshape(tno // 8, 8, tno), axis=0)
+            full = full + single_ref[t, first + j] * x1_ref[:low]
+            full = full + s2_ref[:low] * x2[j:j + 1]
+            return part * full, base_ref[:low] + level_ref[t, first + j]
+
+        for j in range(0, GROUP, 2):
+            top, low_den = pieces(j)
+            other, other_den = pieces(j + 1)
+            term = (top * other_den + other * low_den) / (low_den * other_den)
+            total = total + jnp.sum(term.reshape(low // 8, 8, tno), axis=0)
         acc_ref[...] = total
-        x0_ref[...] = pltpu.roll(x0, tno - GROUP, 1)
-
-    out_ref[...] = jnp.broadcast_to(jnp.sum(acc_ref[...]), out_ref.shape)
+        x0_ref[:low] = pltpu.roll(x0, tno - GROUP, 1)
+
+
+def padded_to(size):
+    return (size + 127) // 128 * 128
 
 
 def triplet_energies(
@@ -100,7 +135,7 @@
 
     out = pl.pallas_call(
         triplet_kernel,
-        out_shape=jax.ShapeDtypeStruct((trips, 1, 128), jnp.float32),
+        out_shape=jax.ShapeDtypeStruct((1, padded_to(trips)), jnp.float32),
         grid_spec=pltpu.PrefetchScalarGridSpec(
             num_scalar_prefetch=5,
             grid=(trips,),
@@ -113,7 +148,7 @@
                 own_spec((3, tno)),
                 own_spec((1, tno)),
             ],
-            out_specs=own_spec((1, 128)),
+            out_specs=pl.BlockSpec((1, padded_to(trips)), lambda t, *_: (0, 0)),
             scratch_shapes=[
                 pltpu.VMEM((tno, 3 * tno), jnp.float32),
                 pltpu.VMEM((tno, 3 * tno), jnp.bfloat16),
@@ -129,7 +164,7 @@
         flat_coeff, flat_coeff, flat_coeff, flat_paired, flat_paired, flat_paired,
         tno_coeff, left, right, singles, levels[:, None, :],
     )
-    return out[:, 0]
+    return out
 
 
 MESH = pl.DeviceIdType.MESH
@@ -187,6 +222,17 @@
     )(block)
 
 
+def partner(me, d, count, sign=1):
+    if count & (count - 1):
+        return lax.rem(me + sign * d + count, count)
+    other, bit = me, 1
+    while bit < count:
+        if d & bit:
+            other = other + bit * (1 - 2 * lax.rem(me // bit, 2))
+        bit *= 2
+    return other
+
+
 def exchange_kernel(
     count, coeff_ref, block_ref, got_coeff, got_block,
     keep_coeff, keep_block, send_sem, recv_sem, pass_sem, land_sem, local_sem,
@@ -205,7 +251,7 @@
     pl.semaphore_wait(barrier, count)
 
     def send(d, k):
-        other = lax.rem(me + d, count)
+        other = partner(me, d, count)
         return pltpu.make_async_remote_copy(
             src_ref=(coeff_ref, block_ref)[k].at[other],
             dst_ref=(got_coeff, got_block)[k].at[rep, me],
@@ -216,7 +262,7 @@
         )
 
     def forward(d, k):
-        origin = lax.rem(me - d + count, count)
+        origin = partner(me, d, count, -1)
         return pltpu.make_async_remote_copy(
             src_ref=(got_coeff, got_block)[k].at[rep, origin],
             dst_ref=(got_coeff, got_block)[k].at[rep, origin],
@@ -226,7 +272,7 @@
             device_id_type=MESH,
         )
 
-    far_first = sorted(range(1, count), key=lambda d: (-min(d, count - d), d))
+    far_first = list(range(count - 1, 0, -1))
     for d in far_first:
         for k in (1, 0):
             send(d, k).start()
@@ -253,14 +299,10 @@
             send(d, k).wait_recv()
             forward(d, k).start()
 
-    @pl.loop(1, count)
-    def _(d):
+    for d in range(count):
         for k in range(2):
-            send(d, k).wait_send()
-
-    @pl.loop(0, count)
-    def _(d):
-        for k in range(2):
+            if d:
+                send(d, k).wait_send()
             forward(d, k).wait()
 
 
@@ -354,9 +396,9 @@
     ref_count = 3 * trips
     capacity = (2 * ref_count + owner_count - 1) // owner_count
 
-    padded = jnp.pad(triplet_pairs, ((0, 0), (0, 128 - 3)))
-    shared = share(padded, 0)[:, :, :3]
-    ids = shared.reshape(owner_count, 2 * ref_count)
+    flat = triplet_pairs.reshape(1, ref_count)
+    flat = jnp.pad(flat, ((0, 0), (0, padded_to(ref_count) - ref_count)))
+    ids = share(flat, 0)[:, 0, :ref_count].reshape(owner_count, 2 * ref_count)
     mine = (ids // pair_dev == me).astype(jnp.float32)
     spot = jnp.arange(2 * ref_count, dtype=jnp.int32)
     before = (spot[:, None] < spot[None, :]).astype(jnp.float32)
@@ -386,13 +428,13 @@
         got_block.reshape(2, -1, pno // 2, 2 * pno),
         tno_coeff, int_left, int_right, singles, tno_energy, gap,
     )
-    everyone = share(energies, 2)[:, :, 0].reshape(-1)
+    everyone = share(energies, 2)[:, 0, :trips].reshape(-1)
     owned = jnp.arange(pair_dev, dtype=jnp.int32) + me * pair_dev
     shares = jnp.repeat(everyone / 3.0, 3)
     pair_energy = jnp.sum(
         jnp.where(ids.reshape(-1)[None, :] == owned[:, None], shares[None, :], 0.0), axis=1
     )
-    return (energies[:, 0], pair_energy)
+    return (energies[0, :trips], pair_energy)
 
 
 def solution(mesh):

time: 199 us -> 198 us (level); the launches traced: 199 us -> 200 us
  Pallas kernels: 182 us -> 186 us
  local copies, waits for them, and re-layouts: 10.6 us -> 7.88 us
    pallas_call x1, Pallas kernels: 80.1 us -> 93.9 us  [exchange(): pl.pallas_call(functools.partial(exchange_kernel, count), out_shape=shape...]
    pallas_call x2, Pallas kernels: 43.5 us -> 36.3 us  [share(): pl.pallas_call(functools.partial(share_kernel, count, reps), out_shape=ja...]
    pallas_call x1, Pallas kernels: 53.7 us -> 51.2 us  [triplet_energies(): pl.pallas_call(triplet_kernel, out_shape=jax.ShapeDtypeStruct((1, padded_...]
where the time goes in v3:
time: 198 us; the launch traced here: 200 us
  Pallas kernels  186 us (94%)
  local copies, waits for them, and re-layouts  7.88 us (4%)
  other arithmetic  5.6 us (3%)
    pallas_call x1, Pallas kernels, exchange(): pl.pallas_call(functools.partial(exchange_kernel, count), out_shape=shape...  93.9 us
    pallas_call x1, Pallas kernels, triplet_energies(): pl.pallas_call(triplet_kernel, out_shape=jax.ShapeDtypeStruct((1, padded_...  51.2 us
    pallas_call x2, Pallas kernels, share(): pl.pallas_call(functools.partial(share_kernel, count, reps), out_shape=ja...  36.3 us
    pallas_call x1, Pallas kernels, gather_rows(): pl.pallas_call(gather_kernel, out_shape=jax.ShapeDtypeStruct((total, pno,...  4.63 us

profile of v3, /device:TPU:0, one launch (start us, length us, event | category | flops | bytes accessed | tf_op | source)
XLA Modules:
  0.0 200.4 jit_solution(7260164249830890528)
XLA Ops:
  0.6 0.8 copy.18
  1.4 0.1 reshape.185
  1.5 0.5 pad.4.x_ref
  2.0 11.3 %share0.1 = s32[32,1,128]{2,1,0:T(1,128)} custom-call(s32[1,128]{1,0:T(1,128)} %pad.4.x_ref), custom_call_target="tpu_custom_call" | custom-call | tf_op jit(solution)/shard_map/share0/pallas_call | solution.py:211
  13.3 0.8 fusion.9
  14.1 0.1 reshape_squeeze.4
  14.2 0.2 convert_reduce_fusion
  14.4 0.6 dynamic_slice.8.pos_ref
  15.0 0.1 fusion.1
  15.1 0.2 select_reduce_fusion.1
  15.3 0.1 copy.19
  15.4 0.1 reshape.189
  15.5 0.7 iota_compare_fusion
  16.3 2.6 %and_select_fusion = bf16[64,64,64]{2,1,0:T(8,128)(2,1)S(1)} fusion(bf16[64,64,64]{2,1,0:T(8,128)(2,1)} %param.16, bf16[64,64,64]{2,1,0:T(8,128)(2,1)} %param.17, pred[]{:T(512)S(6)} %eq.67, pred[64,64]{1,0:T(8,128)(4,1)S(1)} %iota_compare_fusion), kind=kLoop, calls=%fused_computation.1 | loop fusion | flops 786432 | bytes 1576961 | tf_op jit(solution)/shard_map/jit(_where)/select_n | solution.py:412
  18.9 0.1 fusion.8
  19.0 0.3 pad_maximum_fusion
  19.3 1.3 gather_fusion
  20.6 0.6 reshape.186.row_ref
  21.3 4.6 %gather_rows.1 = bf16[48,64,512]{2,1,0:T(8,128)(2,1)} custom-call(s32[48]{0:T(128)} %reshape.186.row_ref, s32[1]{0:T(128)} %bitcast.3.rep_ref, bf16[64,64,1024]{2,1,0:T(8,128)(2,1)} %coeff_ref.1), custom_call_target="tpu_custom_call" | custom-call | tf_op jit(solution)/shard_map/gather_rows/pallas_call | solution.py:360
  25.9 93.9 %exchange.1 = (bf16[2,16,3,64,512]{4,3,2,1,0:T(8,128)(2,1)}, bf16[2,16,3,32,128]{4,3,2,1,0:T(8,128)(2,1)}) custom-call(bf16[16,3,64,512]{3,2,1,0:T(8,128)(2,1)} %bitcast.29, bf16[16,3,32,128]{3,2,1,0:T(8,128)(2,1)} %bitcast.33), custom_call_target="tpu_custom_call" | custom-call | tf_op jit(solution)/shard_map/exchange/pallas_call | solution.py:312
  119.8 0.0 copy-done
  119.9 0.6 copy.21.sing_ref
  120.5 0.6 slice_bitcast_fusion.single_ref
  121.0 51.2 %triplets.1.x_ref = f32[1,128]{1,0:T(1,128)} custom-call(s32[24]{0:T(128)} %dynamic_slice.8.pos_ref, s32[8]{0:T(128)} %width_ref.1, f32[8]{0:T(128)} %gap_ref.1, f32[8,128]{1,0:T(8,128)} %level_ref.1, f32[8,128]{1,0:T(8,128)} %slice_bitcast_fusion.single_ref, bf16[2,48,64,512]{3,2,1,0:T(8,128)(2,1)} %bitcast.26, bf16[2,48,64,512]{3,2,1,0:T(8,128)(2,1)} %bitcast.27, ...), custom_call_target="tpu_custom_call" | custom-call | tf_op jit(solution)/shard_map/triplets/pallas_call | solution.py:136
  172.2 25.0 %share2.1 = f32[32,1,128]{2,1,0:T(1,128)} custom-call(f32[1,128]{1,0:T(1,128)} %triplets.1.x_ref), custom_call_target="tpu_custom_call" | custom-call | tf_op jit(solution)/shard_map/share2/pallas_call | solution.py:211
  197.3 0.8 multiply_reduce_fusion
  198.0 0.1 div.54
  198.1 0.1 broadcast_in_dim.56
  198.2 0.2 broadcast_in_dim.57
  198.5 0.1 eq.68
  198.5 0.7 select_reduce_fusion
  199.2 1.2 slice_bitcast_fusion.1
  (10 shorter events, 0.1 us)
Async XLA Ops:
  21.3 98.6 %copy-start = (f32[8,3,128]{2,0,1:T(8,128)S(1)}, f32[8,3,128]{2,0,1:T(8,128)}, u32[]{:S(2)}) copy-start(f32[8,3,128]{2,0,1:T(8,128)} %param.21) | copy-start | bytes 36868

commit v4 on v3

--- a/solution.py
+++ b/solution.py
@@ -14,7 +14,7 @@
 def triplet_kernel(
     pos_ref, width_ref, gap_ref, level_ref, single_ref,
     c0, c1, c2, p0, p1, p2, tno_ref, left_ref, right_ref, sing_ref, energy_ref,
-    out_ref, lt_ref, at_ref, rm_ref, base_ref, s2_ref, x0_ref, x1_ref, x2_ref, acc_ref,
+    out_ref, lt_ref, at_ref, rm_ref, base_ref, s2_ref, x0_ref, x1_ref, x2_ref, acc_ref, even_ref, odd_ref,
 ):
     t = pl.program_id(0)
     width = width_ref[t]
@@ -67,7 +67,7 @@
         def _(low=low):
             contract(
                 low, t, width, level_ref, single_ref, sing_ref, lt_ref, at_ref, rm_ref,
-                base_ref, s2_ref, x0_ref, x1_ref, x2_ref, acc_ref,
+                base_ref, s2_ref, x0_ref, x1_ref, x2_ref, acc_ref, even_ref, odd_ref,
             )
 
     @pl.when(t == 0)
@@ -80,41 +80,47 @@
 
 def contract(
     low, t, width, level_ref, single_ref, sing_ref, lt_ref, at_ref, rm_ref,
-    base_ref, s2_ref, x0_ref, x1_ref, x2_ref, acc_ref,
+    base_ref, s2_ref, x0_ref, x1_ref, x2_ref, acc_ref, even_ref, odd_ref,
 ):
     tno = rm_ref.shape[1]
-
-    @pl.loop(0, (width + GROUP - 1) // GROUP)
-    def _(g):
-        first = pl.multiple_of(g * GROUP, GROUP)
+    groups = (width + GROUP - 1) // GROUP
+
+    def multiply(g, conn_ref):
+        first = pl.multiple_of(jnp.minimum(g, tno // GROUP - 1) * GROUP, GROUP)
         rows = lt_ref[pl.ds(first, GROUP), :]
         at = at_ref[:low]
         scaled = [
             at * jnp.broadcast_to(rows[j:j + 1], at.shape).astype(jnp.bfloat16)
             for j in range(GROUP)
         ]
-        conn = jnp.dot(
+        conn_ref[:GROUP * low] = jnp.dot(
             jnp.concatenate(scaled, axis=0), rm_ref[...], preferred_element_type=jnp.float32
         )
+
+    def finish(g, conn_ref):
+        first = pl.multiple_of(g * GROUP, GROUP)
         x2 = x2_ref[pl.ds(first, GROUP), :]
         x0 = x0_ref[:low]
         s0 = sing_ref[0, 0:1]
         total = acc_ref[...]
-
-        def pieces(j):
-            part = conn[j * low:(j + 1) * low]
+        for j in range(GROUP):
+            part = conn_ref[j * low:(j + 1) * low]
             full = part + x0[:, j:j + 1] * s0
             full = full + single_ref[t, first + j] * x1_ref[:low]
             full = full + s2_ref[:low] * x2[j:j + 1]
-            return part * full, base_ref[:low] + level_ref[t, first + j]
-
-        for j in range(0, GROUP, 2):
-            top, low_den = pieces(j)
-            other, other_den = pieces(j + 1)
-            term = (top * other_den + other * low_den) / (low_den * other_den)
+            term = part * full / (base_ref[:low] + level_ref[t, first + j])
             total = total + jnp.sum(term.reshape(low // 8, 8, tno), axis=0)
         acc_ref[...] = total
         x0_ref[:low] = pltpu.roll(x0, tno - GROUP, 1)
+
+    multiply(0, even_ref)
+
+    @pl.loop(0, (groups + 1) // 2)
+    def _(h):
+        multiply(2 * h + 1, odd_ref)
+        finish(2 * h, even_ref)
+        multiply(2 * h + 2, even_ref)
+        finish(2 * h + 1, odd_ref)
 
 
 def padded_to(size):
@@ -155,7 +161,8 @@
                 pltpu.VMEM((3 * tno, tno), jnp.bfloat16),
             ]
             + [pltpu.VMEM((tno, tno), jnp.float32)] * 5
-            + [pltpu.VMEM((8, tno), jnp.float32)],
+            + [pltpu.VMEM((8, tno), jnp.float32)]
+            + [pltpu.VMEM((GROUP * tno, tno), jnp.float32)] * 2,
         ),
         compiler_params=pltpu.CompilerParams(dimension_semantics=("arbitrary",)),
         name="triplets",
@@ -272,7 +279,12 @@
             device_id_type=MESH,
         )
 
-    far_first = list(range(count - 1, 0, -1))
+    far_first = []
+    for i, d in enumerate(range(count - 1, count // 2 - 1, -1)):
+        far_first.append(d)
+        if i % 2 and count // 2 - 1 - i // 2 > 0:
+            far_first.append(count // 2 - 1 - i // 2)
+    far_first += [d for d in range(count // 2 - 1, 0, -1) if d not in far_first]
     for d in far_first:
         for k in (1, 0):
             send(d, k).start()

time: 198 us -> 186 us (0.939); the launches traced: 200 us -> 185 us
  Pallas kernels: 186 us -> 171 us
    pallas_call x2, Pallas kernels: 36.3 us -> 25.1 us  [share(): pl.pallas_call(functools.partial(share_kernel, count, reps), out_shape=ja...]
    pallas_call x1, Pallas kernels: 51.2 us -> 46 us  [triplet_energies(): pl.pallas_call(triplet_kernel, out_shape=jax.ShapeDtypeStruct((1, padded_...]
where the time goes in v4:
time: 186 us; the launch traced here: 185 us
  Pallas kernels  171 us (92%)
  local copies, waits for them, and re-layouts  7.88 us (4%)
  other arithmetic  5.6 us (3%)
    pallas_call x1, Pallas kernels, exchange(): pl.pallas_call(functools.partial(exchange_kernel, count), out_shape=shape...  95.3 us
    pallas_call x1, Pallas kernels, triplet_energies(): pl.pallas_call(triplet_kernel, out_shape=jax.ShapeDtypeStruct((1, padded_...  46 us
    pallas_call x2, Pallas kernels, share(): pl.pallas_call(functools.partial(share_kernel, count, reps), out_shape=ja...  25.1 us
    pallas_call x1, Pallas kernels, gather_rows(): pl.pallas_call(gather_kernel, out_shape=jax.ShapeDtypeStruct((total, pno,...  4.63 us

profile of v4, /device:TPU:0, one launch (start us, length us, event | category | flops | bytes accessed | tf_op | source)
XLA Modules:
  0.0 185.4 jit_solution(6509847760126670257)
XLA Ops:
  0.6 0.8 copy.18
  1.4 0.1 reshape.185
  1.5 0.5 pad.4.x_ref
  2.0 11.3 %share0.1 = s32[32,1,128]{2,1,0:T(1,128)} custom-call(s32[1,128]{1,0:T(1,128)} %pad.4.x_ref), custom_call_target="tpu_custom_call" | custom-call | tf_op jit(solution)/shard_map/share0/pallas_call | solution.py:218
  13.3 0.8 fusion.9
  14.1 0.1 reshape_squeeze.4
  14.2 0.2 convert_reduce_fusion
  14.4 0.6 dynamic_slice.8.pos_ref
  15.0 0.1 fusion.1
  15.1 0.2 select_reduce_fusion.1
  15.3 0.1 copy.19
  15.4 0.1 reshape.189
  15.5 0.7 iota_compare_fusion
  16.3 2.6 %and_select_fusion = bf16[64,64,64]{2,1,0:T(8,128)(2,1)S(1)} fusion(bf16[64,64,64]{2,1,0:T(8,128)(2,1)} %param.16, bf16[64,64,64]{2,1,0:T(8,128)(2,1)} %param.17, pred[]{:T(512)S(6)} %eq.67, pred[64,64]{1,0:T(8,128)(4,1)S(1)} %iota_compare_fusion), kind=kLoop, calls=%fused_computation.1 | loop fusion | flops 786432 | bytes 1576961 | tf_op jit(solution)/shard_map/jit(_where)/select_n | solution.py:424
  18.9 0.1 fusion.8
  19.0 0.3 pad_maximum_fusion
  19.3 1.3 gather_fusion
  20.6 0.6 reshape.186.row_ref
  21.3 4.6 %gather_rows.1 = bf16[48,64,512]{2,1,0:T(8,128)(2,1)} custom-call(s32[48]{0:T(128)} %reshape.186.row_ref, s32[1]{0:T(128)} %bitcast.3.rep_ref, bf16[64,64,1024]{2,1,0:T(8,128)(2,1)} %coeff_ref.1), custom_call_target="tpu_custom_call" | custom-call | tf_op jit(solution)/shard_map/gather_rows/pallas_call | solution.py:372
  25.9 95.3 %exchange.1 = (bf16[2,16,3,64,512]{4,3,2,1,0:T(8,128)(2,1)}, bf16[2,16,3,32,128]{4,3,2,1,0:T(8,128)(2,1)}) custom-call(bf16[16,3,64,512]{3,2,1,0:T(8,128)(2,1)} %bitcast.29, bf16[16,3,32,128]{3,2,1,0:T(8,128)(2,1)} %bitcast.33), custom_call_target="tpu_custom_call" | custom-call | tf_op jit(solution)/shard_map/exchange/pallas_call | solution.py:324
  121.2 0.0 copy-done
  121.2 0.6 copy.21.sing_ref
  121.8 0.6 slice_bitcast_fusion.single_ref
  122.4 46.0 %triplets.1.x_ref = f32[1,128]{1,0:T(1,128)} custom-call(s32[24]{0:T(128)} %dynamic_slice.8.pos_ref, s32[8]{0:T(128)} %width_ref.1, f32[8]{0:T(128)} %gap_ref.1, f32[8,128]{1,0:T(8,128)} %level_ref.1, f32[8,128]{1,0:T(8,128)} %slice_bitcast_fusion.single_ref, bf16[2,48,64,512]{3,2,1,0:T(8,128)(2,1)} %bitcast.26, bf16[2,48,64,512]{3,2,1,0:T(8,128)(2,1)} %bitcast.27, ...), custom_call_target="tpu_custom_call" | custom-call | tf_op jit(solution)/shard_map/triplets/pallas_call | solution.py:142
  168.4 13.8 %share2.1 = f32[32,1,128]{2,1,0:T(1,128)} custom-call(f32[1,128]{1,0:T(1,128)} %triplets.1.x_ref), custom_call_target="tpu_custom_call" | custom-call | tf_op jit(solution)/shard_map/share2/pallas_call | solution.py:218
  182.2 0.8 multiply_reduce_fusion
  183.0 0.1 div.54
  183.1 0.1 broadcast_in_dim.56
  183.2 0.2 broadcast_in_dim.57
  183.4 0.1 eq.68
  183.5 0.7 select_reduce_fusion
  184.2 1.2 slice_bitcast_fusion.1
  (10 shorter events, 0.1 us)
Async XLA Ops:
  21.3 99.9 %copy-start = (f32[8,3,128]{2,0,1:T(8,128)S(1)}, f32[8,3,128]{2,0,1:T(8,128)}, u32[]{:S(2)}) copy-start(f32[8,3,128]{2,0,1:T(8,128)} %param.21) | copy-start | bytes 36868
